TPU v7x, 256 devices: a whole 4x4x8 slice. The times are simulated.
256 devices in a mesh: lev: 4 (over x), wav: 64 (over z, y, core).
Axes of the slice: x: 4, y: 4, z: 8, core: 2. Of those that a mesh axis runs over, the one named last changes fastest.
Arguments:
- grid_field: bfloat16 [128, 640, 1280], P('lev', 'wav'), may hold values from -6 to 6
- legendre: bfloat16 [640, 640, 640], P('wav'), may hold values from -0.25 to 0.25
- wave_of_slot: int32 [640], replicated, may hold values from 0 to 639, each once
- lat_of_row: int32 [640], P('wav'), may hold values from 0 to 639, each once
- analysis: bfloat16 [128, 128], replicated, may hold values from -0.5 to 0.5
- synthesis: bfloat16 [128, 128], replicated, may hold values from -0.5 to 0.5
- mode_rates: float32 [128], replicated, may hold values from 0.05 to 5
- flux_weights: float32 [128], replicated, may hold values from -0.5 to 0.5
- remap_mats: bfloat16 [4, 4096, 128, 128], P('lev', 'wav'), may hold values from -0.5 to 0.5
- pair_dest: int32 [4, 4096, 1], P('lev'), may hold values from 0 to 63; in each aligned block of 64 rows (0 to 63, 64 to 127, ..., all dimensions but the last counted through in order) at most 2 rows name the same one
- pair_src: int32 [4, 4096], P('lev'), may hold values from 0 to 99
- pair_dst: int32 [4, 4096], P('lev'), may hold values from 0 to 47
- ocean_temp: float32 [8, 192, 8192], P(None, 'lev', 'wav'), may hold values from -6 to 6
- diffusivity: float32 [192, 8192], P('lev', 'wav'), may hold values from 0.05 to 0.24
- surface_heat: float32 [192, 8192], P('lev', 'wav'), may hold values from -4 to 4
- land_mask: int32 [192, 8192], P('lev', 'wav'), may hold values 0 or 1
Outputs:
- atm_out: bfloat16 [128, 640, 1280], P('lev', 'wav')
- ocean_out: float32 [8, 192, 8192], P(None, 'lev', 'wav')
- ocean_flux: float32 [192, 8192], P('lev', 'wav')
Inputs may be any that keep to these rules, and one draw needn't show every extreme that they name: `wave_of_slot`: each wavenumber names exactly one slot. `lat_of_row`: each latitude names exactly one row. `pair_dest`: within the pairs of one source owner (aligned blocks of 64 pairs of a level row) no destination column is named more than 2 times.
All inputs are finite; a program needn't handle non-finite values. No bound on the sum of `land_mask` on one device may be relied on, other than what follows from the above.
Results may differ from a plain program's by a relative error of at most 0.015.
Values may be sent and summed in bfloat16 or wider, within the bound.
A program may use at most 128 MiB of HBM per device.

v0:
```python
import functools
import math

import jax
import jax.numpy as jnp
from jax import lax
from jax.experimental import pallas as pl
from jax.experimental.pallas import tpu as pltpu
from jax.sharding import PartitionSpec as P

MESH = pl.DeviceIdType.MESH
F32 = jnp.float32
BF16 = jnp.bfloat16
HIGH = lax.Precision.HIGHEST

SWEEPS = 4
NG = 4
NW = 64
ND = NG * NW
LEV = 32
ROWS = 10
LON = 1280
WAVES = 640
NLEV = 128
COLS = 5
SLOTS = 3
MSG = 16
SENT = 14
PAIRS = 64
OX = 48
OLEV = 8
HALO = 8
EXT = OX + 2 * HALO
FIELDS = OLEV + 3

SIN_POLY = (6.28318528, -41.34168068, 81.60248108, -76.58128818, 39.76072297)


def nt(a, b):
    return lax.dot_general(a, b, (((1,), (1,)), ((), ())), preferred_element_type=F32)


def tn(a, b, precision=None):
    return lax.dot_general(
        a, b, (((0,), (0,)), ((), ())), preferred_element_type=F32, precision=precision
    )


def cos_turns(phase, scale):
    whole = jnp.floor(phase * (1.0 / LON) + 0.5)
    rest = jnp.abs(phase - whole * LON)
    t = (LON / 4 - rest) * (1.0 / LON)
    z = t * t
    c = [scale * v for v in SIN_POLY]
    return t * (c[0] + z * (c[1] + z * (c[2] + z * (c[3] + z * c[4]))))


def swap_blocks(v, lane):
    low = lane < 64
    even = lax.rem(lane // 32, 2) == 0
    a0 = jnp.where(low, v[0], pltpu.roll(v[2], 64, 1))
    a2 = jnp.where(low, pltpu.roll(v[0], 64, 1), v[2])
    a1 = jnp.where(low, v[1], pltpu.roll(v[3], 64, 1))
    a3 = jnp.where(low, pltpu.roll(v[1], 64, 1), v[3])
    return (
        jnp.where(even, a0, pltpu.roll(a1, 32, 1)),
        jnp.where(even, pltpu.roll(a0, 96, 1), a1),
        jnp.where(even, a2, pltpu.roll(a3, 32, 1)),
        jnp.where(even, pltpu.roll(a2, 96, 1), a3),
    )


def lanes(shape):
    return lax.broadcasted_iota(jnp.int32, shape, len(shape) - 1)


def down(row):
    return jnp.broadcast_to(row, (128, 128)).T


def kernel(
    wos_s,
    lat_s,
    field,
    legendre,
    wos_t,
    analysis,
    synthesis,
    rates,
    weights,
    mats,
    pairs,
    temp,
    kappa,
    heat,
    mask,
    atm,
    ocean,
    flux,
    table,
    rows_in,
    wide,
    acc,
    out1,
    in1,
    in2,
    leg,
    cols_f,
    flux_f,
    lhs,
    segs,
    mats_v,
    out3,
    in3,
    edge,
    rows_edge,
    in_rows,
    slab,
    in_slab,
    ext,
    local_sem,
    send1,
    recv1,
    send2,
    recv2,
    send3,
    recv3,
    send4,
    recv4,
):
    g = lax.axis_index("lev")
    w = lax.axis_index("wav")
    me = g * NW + w
    barrier = pltpu.get_barrier_semaphore()

    first_slot = (COLS * g) // 2
    leg_copy = pltpu.make_async_copy(
        legendre.at[pl.ds(first_slot, SLOTS)], leg, local_sem.at[0]
    )
    leg_copy.start()
    mats_copy = pltpu.make_async_copy(mats.at[0], mats_v, local_sem.at[1])
    mats_copy.start()

    def greet(j, c):
        there = lax.rem(w + j, NW)
        for i in range(NG):
            pl.semaphore_signal(
                barrier, inc=1, device_id=(lax.rem(g + i, NG), there), device_id_type=MESH
            )
        return c

    lax.fori_loop(1, NW, greet, 0)
    for i in range(1, NG):
        pl.semaphore_signal(
            barrier, inc=1, device_id=(lax.rem(g + i, NG), w), device_id_type=MESH
        )

    def spread(x, c):
        v = field[x]
        for jt in range(10):
            wide[jt, pl.ds(pl.multiple_of(x * 16, 16), ROWS), :] = v[
                :, jt * 128 : (jt + 1) * 128
            ].astype(F32)
        return c

    lax.fori_loop(0, LEV, spread, 0)
    for r in range(ROWS):
        for jt in range(10):
            rows_in[r * LEV : (r + 1) * LEV, jt * 128 : (jt + 1) * 128] = wide[
                jt, pl.ds(r, LEV, stride=16), :
            ].astype(BF16)
    rows_in[320:384, :] = rows_in[256:320, :]

    ocean_mask = mask[...].astype(F32)
    for k in range(OLEV):
        edge[k] = temp[k] * ocean_mask
    edge[OLEV] = ocean_mask
    edge[OLEV + 1] = kappa[...]
    edge[OLEV + 2] = heat[...]
    lane48 = lanes((OX, 128))
    left = jnp.zeros((OX, 128), F32)
    right = jnp.zeros((OX, 128), F32)
    for k in range(FIELDS):
        here = lane48 // 4 == k
        v = edge[k]
        left = jnp.where(here, pltpu.roll(v, 4 * k, 1) if k else v, left)
        right = jnp.where(here, pltpu.roll(v, (4 * k + 4) % 128, 1), right)
        rows_edge[0, k] = v[:HALO]
        rows_edge[1, k] = v[OX - HALO :]
    slab[0] = left
    slab[1] = right

    up, dn = lax.rem(g + NG - 1, NG), lax.rem(g + 1, NG)
    wl, wr = lax.rem(w + NW - 1, NW), lax.rem(w + 1, NW)

    def ocean_copies():
        c = []
        c.append((rows_edge.at[0], in_rows.at[1], (up, w)))
        c.append((rows_edge.at[1], in_rows.at[0], (dn, w)))
        for side, ww in ((0, wl), (1, wr)):
            c.append((slab.at[side], in_slab.at[1 - side, pl.ds(HALO, OX)], (g, ww)))
            c.append(
                (slab.at[side, pl.ds(0, HALO)], in_slab.at[1 - side, pl.ds(HALO + OX, HALO)], (up, ww))
            )
            c.append(
                (slab.at[side, pl.ds(OX - HALO, HALO)], in_slab.at[1 - side, pl.ds(0, HALO)], (dn, ww))
            )
        return [
            pltpu.make_async_remote_copy(
                src_ref=s, dst_ref=d, send_sem=send4.at[i], recv_sem=recv4.at[i],
                device_id=dev, device_id_type=MESH,
            )
            for i, (s, d, dev) in enumerate(c)
        ]

    lane64 = lanes((NW, 128))

    def make_group(i, c):
        gg = lax.rem(g + i, NG)
        base = pl.multiple_of(gg * (COLS * NW), NW)
        for cl in range(COLS):
            q = gg * COLS + cl
            row = wos_t[pl.ds(q // 2, 1), :]
            m = down(row.astype(F32))[:NW]
            shift = (lax.rem(q, 2) * (LON // 4)).astype(F32)
            scale = math.sqrt(2.0 / LON)
            phase = m * lane64.astype(F32) + shift
            now = cos_turns(phase, scale)
            before = cos_turns(phase - 128.0 * m, scale)
            twice = cos_turns(128.0 * m, 2.0)
            for a in range(10):
                table[pl.ds(base + cl * NW, NW), a * 128 : (a + 1) * 128] = now.astype(BF16)
                now, before = twice * now - before, now
        out = nt(table[pl.ds(base, COLS * NW), :], rows_in[...])
        start = pl.multiple_of(gg * (NW * MSG), NW * MSG)
        prev = None
        for cl in range(COLS):
            o = out[cl * NW : (cl + 1) * NW]
            acc[pl.ds(start + 2 * cl, NW, stride=MSG), :] = o[:, :128]
            acc[pl.ds(start + 2 * cl + 1, NW, stride=MSG), :] = o[:, 128:256]
            if cl % 2 == 0:
                prev = o[:, 256:384]
            if cl % 2 == 1 or cl == COLS - 1:
                acc[pl.ds(start + 10 + cl // 2, NW, stride=MSG), :] = jnp.where(
                    lane64 < 64, prev, o[:, 256:384]
                )
        out1[pl.ds(gg * NW, NW)] = (
            acc[pl.ds(start, NW * MSG), :].reshape(NW, MSG, 128).astype(BF16)
        )

        @pl.when(i == 0)
        def _():
            pl.semaphore_wait(barrier, ND - 1)
            for copy in ocean_copies():
                copy.start()
            in1[me] = out1[me]

        def send(j, c):
            there = lax.rem(w + j, NW)
            pltpu.make_async_remote_copy(
                src_ref=out1.at[gg * NW + there, pl.ds(0, SENT)],
                dst_ref=in1.at[me, pl.ds(0, SENT)],
                send_sem=send1,
                recv_sem=recv1,
                device_id=(gg, there),
                device_id_type=MESH,
            ).start()
            return c

        lax.fori_loop(jnp.where(i == 0, 1, 0), NW, send, 0)
        return c

    lax.fori_loop(0, NG, make_group, 0)

    for copy in ocean_copies():
        copy.wait()
    sub_e = lax.broadcasted_iota(jnp.int32, (EXT, 256), 0)
    lane_e = lanes((EXT, 256))
    inside_rows = jnp.logical_and(
        jnp.logical_or(sub_e >= HALO, g > 0),
        jnp.logical_or(sub_e < HALO + OX, g < NG - 1),
    )
    inside = jnp.logical_and(
        inside_rows,
        jnp.logical_and(
            jnp.logical_or(lane_e < 252, w > 0),
            jnp.logical_or(jnp.logical_or(lane_e < 128, lane_e >= 252), w < NW - 1),
        ),
    )
    lane_m = lanes((EXT, 128))
    for k in range(FIELDS):
        ext[k, :HALO, :128] = in_rows[0, k]
        ext[k, HALO : HALO + OX, :128] = edge[k]
        ext[k, HALO + OX :, :128] = in_rows[1, k]
        from_left = pltpu.roll(in_slab[0], (124 - 4 * k) % 128, 1)
        from_right = pltpu.roll(in_slab[1], (128 - 4 * k) % 128, 1) if k else in_slab[1]
        ext[k, :, 128:] = jnp.where(
            lane_m >= 124, from_left, jnp.where(lane_m < 4, from_right, 0.0)
        )
    e_mask = jnp.where(inside, ext[OLEV], 0.0)
    ext[OLEV] = e_mask
    for k in range(2):
        ext[OLEV + 1 + k] = jnp.where(inside, ext[OLEV + 1 + k], 0.0)

    def level(k, c):
        cur = jnp.where(inside, ext[k], 0.0)
        add = jnp.where(k == 0, 1.0, 0.0).astype(F32) * ext[OLEV + 2]
        for _ in range(SWEEPS):
            lap = (
                pltpu.roll(cur, EXT - 1, 0)
                + pltpu.roll(cur, 1, 0)
                + pltpu.roll(cur, 255, 1)
                + pltpu.roll(cur, 1, 1)
                - 4.0 * cur
            )
            cur = ext[OLEV] * (cur + ext[OLEV + 1] * lap + add)
        ocean[k] = cur[HALO : HALO + OX, :128]
        return c

    lax.fori_loop(0, OLEV, level, 0)

    sub_p = lax.broadcasted_iota(jnp.int32, (PAIRS, PAIRS), 0)
    lane_p = lanes((PAIRS, PAIRS))
    upper = (sub_p < lane_p).astype(BF16)
    dest_all = pairs[0]
    hits = dest_all == w
    rank_in = jnp.dot(hits.astype(BF16), upper, preferred_element_type=F32)
    lane_o = lanes((PAIRS, 128))
    pick_in = []
    for s in range(2):
        chosen_s = jnp.logical_and(hits, rank_in == float(s))
        row_of = jnp.sum(
            jnp.where(chosen_s, pairs[2].astype(F32) + 1.0, 0.0), axis=1, keepdims=True
        )
        pick_in.append((lane_o.astype(F32) + 1.0 == row_of).astype(F32))
    my_dest = pairs[0, pl.ds(w, 1), :]
    my_src = pairs[1, pl.ds(w, 1), :]
    same = sub_p == my_dest
    counts = jnp.dot(same.astype(BF16), upper, preferred_element_type=F32)
    rank_out = jnp.sum(jnp.where(same, counts, 0.0), axis=0, keepdims=True)
    pick_out = [
        jnp.logical_and(same, rank_out == float(s)).astype(F32) for s in range(2)
    ]
    src_row = my_src // 10
    seg_at = (my_src - src_row * 10) * 16 + src_row
    pick_seg = (lax.broadcasted_iota(jnp.int32, (160, PAIRS), 0) == seg_at).astype(BF16)

    degree = lanes((NLEV, WAVES))
    base = (degree * (degree + 1)).astype(F32) / float(WAVES * WAVES)
    rate = down(rates[...])
    weight = down(weights[...])
    damping = 1.0 / (1.0 + jnp.concatenate([rate] * 5, axis=1) * base)
    leg_copy.wait()

    def all_but_one(send_sem, recv_sem, src, dst):
        return pltpu.make_async_remote_copy(
            src_ref=src.at[pl.ds(0, ND - 1), pl.ds(0, SENT)],
            dst_ref=dst.at[pl.ds(0, ND - 1), pl.ds(0, SENT)],
            send_sem=send_sem,
            recv_sem=recv_sem,
            device_id=(g, w),
            device_id_type=MESH,
        )

    def widen(src):
        def step(i, c):
            n = ND // 16
            acc[pl.ds(pl.multiple_of(i * n * MSG, n * MSG), n * MSG), :] = (
                src[pl.ds(i * n, n)].astype(F32).reshape(n * MSG, 128)
            )
            return c

        lax.fori_loop(0, 16, step, 0)

    first = all_but_one(send1, recv1, out1, in1)
    first.wait_send()
    first.wait_recv()
    widen(in1)

    def at(ref, start, n, stride):
        return ref[pl.ds(start, n, stride=stride), :]

    for cl in range(COLS):
        for t in range(2):
            v = [at(acc, k * NW * MSG + 2 * cl + t, NW, MSG) for k in range(NG)]
            for q, out in enumerate(swap_blocks(v, lane64)):
                cols_f[pl.ds(cl * WAVES + 4 * t + q, NW, stride=ROWS), :] = out
    for p in range(3):
        v = [at(acc, k * NW * MSG + 10 + p, NW, MSG) for k in range(NG)]
        for q, out in enumerate(swap_blocks(v, lane64)):
            if 2 * p + q // 2 < COLS:
                cols_f[pl.ds((2 * p + q // 2) * WAVES + 8 + q % 2, NW, stride=ROWS), :] = out

    odd = lax.rem(g, 2)

    def column(cl, c):
        here = pl.ds(pl.multiple_of(cl * WAVES, WAVES), WAVES)
        table_of = leg[(odd + cl) // 2]
        m = wos_s[w * 10 + (COLS * g + cl) // 2]
        spectra = jnp.dot(
            cols_f[here, :].T.astype(BF16), table_of, preferred_element_type=F32
        )
        spectra = jnp.where(degree >= m, spectra, 0.0).astype(BF16)
        modal = jnp.dot(analysis[...], spectra, preferred_element_type=F32)
        modal = (modal * damping).astype(BF16)
        solved = jnp.dot(synthesis[...], modal, preferred_element_type=F32).astype(BF16)
        flux_coef = jnp.concatenate(
            [
                jnp.sum(
                    weight * solved[:, b * 128 : (b + 1) * 128].astype(F32),
                    axis=0,
                    keepdims=True,
                )
                for b in range(5)
            ],
            axis=1,
        )
        right = jnp.concatenate(
            [solved, jnp.broadcast_to(flux_coef, (128, WAVES)).astype(BF16)], axis=0
        )
        back = nt(table_of, right)
        cols_f[here, :] = back[:, :128]
        flux_f[here, :] = back[:, 128:]
        return c

    lax.fori_loop(0, COLS, column, 0)

    for cl in range(COLS):
        for t in range(2):
            v = [at(cols_f, cl * WAVES + 4 * t + q, NW, ROWS) for q in range(NG)]
            for k, out in enumerate(swap_blocks(v, lane64)):
                acc[pl.ds(k * NW * MSG + 2 * cl + t, NW, stride=MSG), :] = out
    fluxes = jnp.zeros((NW, 128), F32)
    for cl in range(COLS):
        for r in range(ROWS):
            fluxes = jnp.where(
                lane64 == 64 + cl * ROWS + r, at(flux_f, cl * WAVES + r, NW, ROWS), fluxes
            )
    for p in range(3):
        v = []
        for q in range(4):
            cl = min(2 * p + q // 2, COLS - 1)
            v.append(at(cols_f, cl * WAVES + 8 + q % 2, NW, ROWS))
        for k, out in enumerate(swap_blocks(v, lane64)):
            if p == 2:
                out = jnp.where(lane64 < 64, out, fluxes)
            acc[pl.ds(k * NW * MSG + 10 + p, NW, stride=MSG), :] = out

    def send_group(i, c):
        gg = lax.rem(g + i, NG)
        start = pl.multiple_of(gg * (NW * MSG), NW * MSG)
        out1[pl.ds(gg * NW, NW)] = (
            acc[pl.ds(start, NW * MSG), :].reshape(NW, MSG, 128).astype(BF16)
        )

        @pl.when(i == 0)
        def _():
            in2[me] = out1[me]

        def send(j, c):
            there = lax.rem(w + j, NW)
            pltpu.make_async_remote_copy(
                src_ref=out1.at[gg * NW + there, pl.ds(0, SENT)],
                dst_ref=in2.at[me, pl.ds(0, SENT)],
                send_sem=send2,
                recv_sem=recv2,
                device_id=(gg, there),
                device_id_type=MESH,
            ).start()
            return c

        lax.fori_loop(jnp.where(i == 0, 1, 0), NW, send, 0)
        return c

    lax.fori_loop(0, NG, send_group, 0)
    mats_copy.wait()
    second = all_but_one(send2, recv2, out1, in2)
    second.wait_send()
    second.wait_recv()
    widen(in2)

    for k in range(NG):
        f12 = at(acc, k * NW * MSG + 12, NW, MSG)
        for cl in range(COLS):
            rows = pl.ds((k * COLS + cl) * NW, NW)
            for t in range(2):
                lhs[rows, t * 128 : (t + 1) * 128] = at(
                    acc, k * NW * MSG + 2 * cl + t, NW, MSG
                ).astype(BF16)
            v = at(acc, k * NW * MSG + 10 + cl // 2, NW, MSG) if cl < 4 else f12
            if cl % 2 == 1:
                v = pltpu.roll(v, 64, 1)
            f = pltpu.roll(f12, 128 - cl * ROWS, 1) if cl else f12
            lhs[rows, 256:384] = jnp.where(
                lane64 < 64, v, jnp.where(lane64 < 64 + ROWS, f, 0.0)
            ).astype(BF16)
    last = tn(lhs[:, 256:384], table[...])
    for r in range(2):
        for jt in range(10):
            wide[jt, pl.ds(8 + r, LEV, stride=16), :] = last[
                r * LEV : (r + 1) * LEV, jt * 128 : (jt + 1) * 128
            ]
    for jt in range(10):
        segs[jt * 16 : (jt + 1) * 16, :] = last[64:80, jt * 128 : (jt + 1) * 128].astype(BF16)
    chosen = tn(pick_seg, segs[...]).astype(BF16)
    sub8 = lax.broadcasted_iota(jnp.int32, (8, 128), 0)
    parts = []
    for b in range(PAIRS // 8):
        total = jnp.zeros((8, 128), F32)
        eight = chosen[b * 8 : (b + 1) * 8]
        for u in range(8):
            total = jnp.where(sub8 == u, nt(eight, mats_v[b * 8 + u]), total)
        parts.append(total)
    products = jnp.concatenate(parts, axis=0)
    for s in range(2):
        out3[pl.ds(s, NW, stride=8), :] = jnp.dot(
            pick_out[s], products, precision=HIGH, preferred_element_type=F32
        )
    in3[pl.ds(pl.multiple_of(w * 8, 8), 8), :] = out3[pl.ds(pl.multiple_of(w * 8, 8), 8), :]

    def send_flux(j, c):
        there = lax.rem(w + j, NW)
        pltpu.make_async_remote_copy(
            src_ref=out3.at[pl.ds(pl.multiple_of(there * 8, 8), 8)],
            dst_ref=in3.at[pl.ds(pl.multiple_of(w * 8, 8), 8)],
            send_sem=send3,
            recv_sem=recv3,
            device_id=(g, there),
            device_id_type=MESH,
        ).start()
        return c

    lax.fori_loop(1, NW, send_flux, 0)

    for t in range(2):
        main = tn(lhs[:, t * 128 : (t + 1) * 128], table[...])
        for q in range(4):
            for jt in range(10):
                wide[jt, pl.ds(4 * t + q, LEV, stride=16), :] = main[
                    q * LEV : (q + 1) * LEV, jt * 128 : (jt + 1) * 128
                ]
    sub16 = lax.broadcasted_iota(jnp.int32, (16, 128), 0)
    mu = jnp.zeros((16, 128), F32)
    for r in range(ROWS):
        mu = jnp.where(sub16 == r, lat_s[r].astype(F32), mu)
    mu = -cos_turns(mu + 0.5, 1.0)
    mu = mu[:ROWS]

    def finish(x, c):
        v = field[x].astype(F32)
        for jt in range(10):
            cut = slice(jt * 128, (jt + 1) * 128)
            grid = wide[jt, pl.ds(pl.multiple_of(x * 16, 16), ROWS), :]
            atm[x, :, cut] = (grid * (1.0 + v[:, cut] * mu)).astype(BF16)
        return c

    lax.fori_loop(0, LEV, finish, 0)

    third = pltpu.make_async_remote_copy(
        src_ref=out3.at[pl.ds(0, (NW - 1) * 8)],
        dst_ref=in3.at[pl.ds(0, (NW - 1) * 8)],
        send_sem=send3,
        recv_sem=recv3,
        device_id=(g, w),
        device_id_type=MESH,
    )
    third.wait_send()
    third.wait_recv()
    summed = jnp.zeros((128, 128), F32)
    for s in range(2):
        summed = summed + tn(pick_in[s], at(in3, s, NW, 8), HIGH)
    flux[...] = summed[:OX]


def per_device(
    grid_field,
    legendre,
    wave_of_slot,
    lat_of_row,
    analysis,
    synthesis,
    mode_rates,
    flux_weights,
    remap_mats,
    pair_dest,
    pair_src,
    pair_dst,
    ocean_temp,
    diffusivity,
    surface_heat,
    land_mask,
):
    waves = jnp.pad(wave_of_slot.reshape(NW, 10).T, ((0, 6), (0, 64)))
    pairs = jnp.stack([pair_dest.reshape(-1), pair_src.reshape(-1), pair_dst.reshape(-1)])
    pairs = pairs.reshape(3, NW, PAIRS)
    smem = pl.BlockSpec(memory_space=pltpu.SMEM)
    vmem = pl.BlockSpec(memory_space=pltpu.VMEM)
    anys = pl.BlockSpec(memory_space=pl.ANY)
    return pl.pallas_call(
        kernel,
        out_shape=(
            jax.ShapeDtypeStruct((LEV, ROWS, LON), BF16),
            jax.ShapeDtypeStruct((OLEV, OX, 128), F32),
            jax.ShapeDtypeStruct((OX, 128), F32),
        ),
        in_specs=[smem, smem, vmem, anys, vmem, vmem, vmem, vmem, vmem, anys]
        + [vmem] * 5,
        out_specs=(vmem, vmem, vmem),
        scratch_shapes=[
            pltpu.VMEM((LON, LON), BF16),
            pltpu.VMEM((384, LON), BF16),
            pltpu.VMEM((10, LEV * 16, 128), F32),
            pltpu.VMEM((ND * MSG, 128), F32),
            pltpu.VMEM((ND, MSG, 128), BF16),
            pltpu.VMEM((ND, MSG, 128), BF16),
            pltpu.VMEM((ND, MSG, 128), BF16),
            pltpu.VMEM((SLOTS, WAVES, WAVES), BF16),
            pltpu.VMEM((COLS * WAVES, 128), F32),
            pltpu.VMEM((COLS * WAVES, 128), F32),
            pltpu.VMEM((LON, 384), BF16),
            pltpu.VMEM((160, 128), BF16),
            pltpu.VMEM((PAIRS, 128, 128), BF16),
            pltpu.VMEM((NW * 8, 128), F32),
            pltpu.VMEM((NW * 8, 128), F32),
            pltpu.VMEM((FIELDS, OX, 128), F32),
            pltpu.VMEM((2, FIELDS, HALO, 128), F32),
            pltpu.VMEM((2, FIELDS, HALO, 128), F32),
            pltpu.VMEM((2, OX, 128), F32),
            pltpu.VMEM((2, EXT, 128), F32),
            pltpu.VMEM((FIELDS, EXT, 256), F32),
            pltpu.SemaphoreType.DMA((2,)),
            pltpu.SemaphoreType.DMA(()),
            pltpu.SemaphoreType.DMA(()),
            pltpu.SemaphoreType.DMA(()),
            pltpu.SemaphoreType.DMA(()),
            pltpu.SemaphoreType.DMA(()),
            pltpu.SemaphoreType.DMA(()),
            pltpu.SemaphoreType.DMA((8,)),
            pltpu.SemaphoreType.DMA((8,)),
        ],
        compiler_params=pltpu.CompilerParams(
            collective_id=0, has_side_effects=True, vmem_limit_bytes=60 * 1024 * 1024
        ),
        name="step",
    )(
        wave_of_slot,
        lat_of_row,
        grid_field,
        legendre,
        waves,
        analysis,
        synthesis,
        mode_rates.reshape(1, NLEV),
        flux_weights.reshape(1, NLEV),
        remap_mats,
        pairs,
        ocean_temp,
        diffusivity,
        surface_heat,
        land_mask,
    )


def solution(mesh):
    return jax.shard_map(
        per_device,
        mesh=mesh,
        in_specs=(
            P("lev", "wav", None),
            P("wav", None, None),
            P(),
            P("wav"),
            P(),
            P(),
            P(),
            P(),
            P("lev", "wav", None, None),
            P("lev", None, None),
            P("lev", None),
            P("lev", None),
            P(None, "lev", "wav"),
            P("lev", "wav"),
            P("lev", "wav"),
            P("lev", "wav"),
        ),
        out_specs=(P("lev", "wav", None), P(None, "lev", "wav"), P("lev", "wav")),
        check_vma=False,
    )
```

profile of v0, /device:TPU:1, one launch (start us, length us, event | category | flops | bytes accessed | tf_op | source)
XLA Modules:
  0.0 101.1 jit_solution(135964839222327935)
XLA Ops:
  0.6 0.5 broadcast.11
  1.1 1.4 %reduce.11 = s32[4096]{0:T(1024)S(1)} reduce(s32[1,4096,1]{1,2,0:T(1,128)} %param.25, s32[]{:T(128)} %broadcast.11), dimensions={0,2}, to_apply=%param.25.reduce_sub_computation.3 | reduce | bytes 32772 | tf_op args[9]
  2.5 0.1 stack.9
  2.6 1.4 %reduce.10 = s32[4096]{0:T(1024)S(1)} reduce(s32[1,4096]{1,0:T(1,128)} %param.26, s32[]{:T(128)} %broadcast.11), dimensions={0}, to_apply=%param.26.reduce_sub_computation.3 | reduce | bytes 32772 | tf_op args[10]
  4.0 1.4 %reduce.9 = s32[4096]{0:T(1024)S(1)} reduce(s32[1,4096]{1,0:T(1,128)} %param.27, s32[]{:T(128)} %broadcast.11), dimensions={0}, to_apply=%param.27.reduce_sub_computation.3 | reduce | bytes 32772 | tf_op args[11]
  5.4 0.1 stack.11
  5.5 0.1 stack.10
  5.6 0.7 pad_add_fusion.pairs
  6.2 0.8 reshape.20
  7.0 0.1 copy.21
  7.1 0.6 pad.4.wos_t
  7.7 2.7 %copy.22.field = bf16[32,10,1280]{2,1,0:T(8,128)(2,1)} copy(bf16[32,10,1280]{2,0,1:T(8,128)(2,1)} %param.16) | data formatting | bytes 1638400 | tf_op args[0]
  10.4 86.9 %step.1 = (bf16[32,10,1280]{2,1,0:T(8,128)(2,1)}, f32[8,48,128]{2,1,0:T(8,128)}, f32[48,128]{1,0:T(8,128)}) custom-call(s32[640]{0:T(1024)} %wos_s.1, s32[10]{0:T(128)} %lat_s.1, bf16[32,10,1280]{2,1,0:T(8,128)(2,1)} %copy.22.field, bf16[10,640,640]{2,1,0:T(8,128)(2,1)} %legendre.1, s32[16,128]{1,0:T(8,128)} %pad.4.wos_t, bf16[128,128]{1,0:T(8,128)(2,1)} %analysis.1, ...), custom_call_target="tpu_custom_call" | custom-call | tf_op jit(solution)/shard_map/step/pallas_call | solution.py:599
  97.3 0.0 copy-start
  97.3 0.0 copy-start.1
  97.3 2.5 %copy.23 = bf16[32,10,1280]{2,0,1:T(8,128)(2,1)} copy(bf16[32,10,1280]{2,1,0:T(8,128)(2,1)} %get-tuple-element.6) | data formatting | bytes 1638400 | tf_op jit(solution)/shard_map/step/pallas_call | solution.py:599
  99.8 0.0 copy-done
  99.8 0.7 copy.26
  100.5 0.0 copy-done.1
  100.5 0.6 copy.27
Async XLA Ops:
  97.3 2.5 %copy-start = (f32[8,48,128]{2,1,0:T(8,128)S(1)}, f32[8,48,128]{2,1,0:T(8,128)}, u32[]{:S(2)}) copy-start(f32[8,48,128]{2,1,0:T(8,128)} %get-tuple-element.13) | copy-start | bytes 589828
  97.3 3.2 %copy-start.1 = (f32[48,128]{1,0:T(8,128)S(1)}, f32[48,128]{1,0:T(8,128)}, u32[]{:S(2)}) copy-start(f32[48,128]{1,0:T(8,128)} %get-tuple-element.14) | copy-start | bytes 73732
where the time goes:
time: 102 us; the launch traced here: 101 us
  Pallas kernels  86.9 us (85%)
  local copies, waits for them, and re-layouts  8.68 us (9%)
  other arithmetic  4.86 us (5%)
    pallas_call x1, Pallas kernels, per_device(): pl.pallas_call(kernel, out_shape=(jax.ShapeDtypeStruct((LEV, ROWS, LON),...  86.9 us
    unnamed x8, local copies, waits for them, and re-layouts  4.48 us
    unnamed x3, other arithmetic  4.21 us
    pallas_call x1, local copies, waits for them, and re-layouts, per_device(): pl.pallas_call(kernel, out_shape=(jax.ShapeDtypeStruct((LEV, ROWS, LON),...  2.48 us

commit v1 on v0

--- a/solution.py
+++ b/solution.py
@@ -83,13 +83,15 @@
     lat_s,
     field,
     legendre,
-    wos_t,
+    wos_v,
     analysis,
     synthesis,
     rates,
     weights,
     mats,
-    pairs,
+    p_dest,
+    p_src,
+    p_dst,
     temp,
     kappa,
     heat,
@@ -99,7 +101,7 @@
     flux,
     table,
     rows_in,
-    wide,
+    waves,
     acc,
     out1,
     in1,
@@ -118,6 +120,7 @@
     slab,
     in_slab,
     ext,
+    ready,
     local_sem,
     send1,
     recv1,
@@ -141,35 +144,36 @@
     mats_copy = pltpu.make_async_copy(mats.at[0], mats_v, local_sem.at[1])
     mats_copy.start()
 
-    def greet(j, c):
-        there = lax.rem(w + j, NW)
-        for i in range(NG):
-            pl.semaphore_signal(
-                barrier, inc=1, device_id=(lax.rem(g + i, NG), there), device_id_type=MESH
-            )
-        return c
-
-    lax.fori_loop(1, NW, greet, 0)
-    for i in range(1, NG):
+    low = lax.rem(w, 4)
+    high = w // 4
+    for i in range(NG):
+        for j in range(4):
+            if i or j:
+                pl.semaphore_signal(
+                    barrier,
+                    inc=1,
+                    device_id=(lax.rem(g + i, NG), high * 4 + lax.rem(low + j, 4)),
+                    device_id_type=MESH,
+                )
+    for j in range(1, 16):
         pl.semaphore_signal(
-            barrier, inc=1, device_id=(lax.rem(g + i, NG), w), device_id_type=MESH
-        )
-
-    def spread(x, c):
-        v = field[x]
-        for jt in range(10):
-            wide[jt, pl.ds(pl.multiple_of(x * 16, 16), ROWS), :] = v[
-                :, jt * 128 : (jt + 1) * 128
-            ].astype(F32)
-        return c
-
-    lax.fori_loop(0, LEV, spread, 0)
+            barrier,
+            inc=1,
+            device_id=(g, lax.rem(high + j, 16) * 4 + low),
+            device_id_type=MESH,
+        )
+
     for r in range(ROWS):
-        for jt in range(10):
-            rows_in[r * LEV : (r + 1) * LEV, jt * 128 : (jt + 1) * 128] = wide[
-                jt, pl.ds(r, LEV, stride=16), :
-            ].astype(BF16)
-    rows_in[320:384, :] = rows_in[256:320, :]
+        rows_in[r * LEV : (r + 1) * LEV, :] = field[r]
+    rows_in[320:352, :] = field[8]
+    rows_in[352:384, :] = field[9]
+
+    sub_w = lax.broadcasted_iota(jnp.int32, (NW, WAVES), 0)
+    at_slot = lanes((NW, WAVES)) - 10 * sub_w
+    all_waves = jnp.broadcast_to(wos_v[...].reshape(1, WAVES).astype(F32), (NW, WAVES))
+    for k in range(10):
+        m = jnp.sum(jnp.where(at_slot == k, all_waves, 0.0), axis=1, keepdims=True)
+        waves[k] = jnp.broadcast_to(m, (NW, 128))
 
     ocean_mask = mask[...].astype(F32)
     for k in range(OLEV):
@@ -220,8 +224,7 @@
         base = pl.multiple_of(gg * (COLS * NW), NW)
         for cl in range(COLS):
             q = gg * COLS + cl
-            row = wos_t[pl.ds(q // 2, 1), :]
-            m = down(row.astype(F32))[:NW]
+            m = waves[q // 2]
             shift = (lax.rem(q, 2) * (LON // 4)).astype(F32)
             scale = math.sqrt(2.0 / LON)
             phase = m * lane64.astype(F32) + shift
@@ -231,6 +234,17 @@
             for a in range(10):
                 table[pl.ds(base + cl * NW, NW), a * 128 : (a + 1) * 128] = now.astype(BF16)
                 now, before = twice * now - before, now
+        @pl.when(i == 0)
+        def _():
+            pl.semaphore_wait(barrier, 30)
+            for j in range(1, 16):
+                pl.semaphore_signal(
+                    ready,
+                    inc=1,
+                    device_id=(g, lax.rem(high + j, 16) * 4 + low),
+                    device_id_type=MESH,
+                )
+
         out = nt(table[pl.ds(base, COLS * NW), :], rows_in[...])
         start = pl.multiple_of(gg * (NW * MSG), NW * MSG)
         prev = None
@@ -250,7 +264,7 @@
 
         @pl.when(i == 0)
         def _():
-            pl.semaphore_wait(barrier, ND - 1)
+            pl.semaphore_wait(ready, 15)
             for copy in ocean_copies():
                 copy.start()
             in1[me] = out1[me]
@@ -319,24 +333,31 @@
 
     lax.fori_loop(0, OLEV, level, 0)
 
-    sub_p = lax.broadcasted_iota(jnp.int32, (PAIRS, PAIRS), 0)
-    lane_p = lanes((PAIRS, PAIRS))
-    upper = (sub_p < lane_p).astype(BF16)
-    dest_all = pairs[0]
-    hits = dest_all == w
+    sub_p = lax.broadcasted_iota(jnp.int32, (128, 128), 0)
+    lane_p = lanes((128, 128))
+    upper = jnp.logical_and(sub_p < lane_p, sub_p // PAIRS == lane_p // PAIRS).astype(BF16)
+    hits = p_dest[...] == w
     rank_in = jnp.dot(hits.astype(BF16), upper, preferred_element_type=F32)
-    lane_o = lanes((PAIRS, 128))
-    pick_in = []
-    for s in range(2):
-        chosen_s = jnp.logical_and(hits, rank_in == float(s))
-        row_of = jnp.sum(
-            jnp.where(chosen_s, pairs[2].astype(F32) + 1.0, 0.0), axis=1, keepdims=True
-        )
-        pick_in.append((lane_o.astype(F32) + 1.0 == row_of).astype(F32))
-    my_dest = pairs[0, pl.ds(w, 1), :]
-    my_src = pairs[1, pl.ds(w, 1), :]
-    same = sub_p == my_dest
-    counts = jnp.dot(same.astype(BF16), upper, preferred_element_type=F32)
+    lane_h = lanes((NW // 2, 128))
+    dst_in = p_dst[...].astype(F32) + 1.0
+    pick_in = {}
+    for half in range(2):
+        mine = jnp.logical_and(hits, lane_h // PAIRS == half)
+        for s in range(2):
+            chosen_s = jnp.logical_and(mine, rank_in == float(s))
+            row_of = jnp.sum(jnp.where(chosen_s, dst_in, 0.0), axis=1, keepdims=True)
+            pick_in[half, s] = (lane_h.astype(F32) + 1.0 == row_of).astype(F32)
+
+    def my_row(ref):
+        row = ref[pl.ds(w // 2, 1), :]
+        return jnp.where(lax.rem(w, 2) == 1, pltpu.roll(row, PAIRS, 1), row)[:, :PAIRS]
+
+    my_dest = my_row(p_dest)
+    my_src = my_row(p_src)
+    same = lax.broadcasted_iota(jnp.int32, (NW, PAIRS), 0) == my_dest
+    counts = jnp.dot(
+        same.astype(BF16), upper[:PAIRS, :PAIRS], preferred_element_type=F32
+    )
     rank_out = jnp.sum(jnp.where(same, counts, 0.0), axis=0, keepdims=True)
     pick_out = [
         jnp.logical_and(same, rank_out == float(s)).astype(F32) for s in range(2)
@@ -495,11 +516,18 @@
                 lane64 < 64, v, jnp.where(lane64 < 64 + ROWS, f, 0.0)
             ).astype(BF16)
     last = tn(lhs[:, 256:384], table[...])
-    for r in range(2):
+    mu = [
+        -cos_turns(jnp.full((LEV, 128), lat_s[r], jnp.int32).astype(F32) + 0.5, 1.0)
+        for r in range(ROWS)
+    ]
+
+    def finish(r, grid):
         for jt in range(10):
-            wide[jt, pl.ds(8 + r, LEV, stride=16), :] = last[
-                r * LEV : (r + 1) * LEV, jt * 128 : (jt + 1) * 128
-            ]
+            cut = slice(jt * 128, (jt + 1) * 128)
+            atm[r, :, cut] = (
+                grid[:, cut] * (1.0 + field[r, :, cut].astype(F32) * mu[r])
+            ).astype(BF16)
+
     for jt in range(10):
         segs[jt * 16 : (jt + 1) * 16, :] = last[64:80, jt * 128 : (jt + 1) * 128].astype(BF16)
     chosen = tn(pick_seg, segs[...]).astype(BF16)
@@ -532,29 +560,12 @@
 
     lax.fori_loop(1, NW, send_flux, 0)
 
+    for r in range(2):
+        finish(8 + r, last[r * LEV : (r + 1) * LEV])
     for t in range(2):
         main = tn(lhs[:, t * 128 : (t + 1) * 128], table[...])
         for q in range(4):
-            for jt in range(10):
-                wide[jt, pl.ds(4 * t + q, LEV, stride=16), :] = main[
-                    q * LEV : (q + 1) * LEV, jt * 128 : (jt + 1) * 128
-                ]
-    sub16 = lax.broadcasted_iota(jnp.int32, (16, 128), 0)
-    mu = jnp.zeros((16, 128), F32)
-    for r in range(ROWS):
-        mu = jnp.where(sub16 == r, lat_s[r].astype(F32), mu)
-    mu = -cos_turns(mu + 0.5, 1.0)
-    mu = mu[:ROWS]
-
-    def finish(x, c):
-        v = field[x].astype(F32)
-        for jt in range(10):
-            cut = slice(jt * 128, (jt + 1) * 128)
-            grid = wide[jt, pl.ds(pl.multiple_of(x * 16, 16), ROWS), :]
-            atm[x, :, cut] = (grid * (1.0 + v[:, cut] * mu)).astype(BF16)
-        return c
-
-    lax.fori_loop(0, LEV, finish, 0)
+            finish(4 * t + q, main[q * LEV : (q + 1) * LEV])
 
     third = pltpu.make_async_remote_copy(
         src_ref=out3.at[pl.ds(0, (NW - 1) * 8)],
@@ -567,9 +578,26 @@
     third.wait_send()
     third.wait_recv()
     summed = jnp.zeros((128, 128), F32)
-    for s in range(2):
-        summed = summed + tn(pick_in[s], at(in3, s, NW, 8), HIGH)
+    for half in range(2):
+        for s in range(2):
+            summed = summed + tn(
+                pick_in[half, s], at(in3, half * 8 + s, NW // 2, 16), HIGH
+            )
     flux[...] = summed[:OX]
+
+
+def hand_over(atm_in, ocean_in, flux_in, atm, ocean, flux, atm_v, ocean_v, flux_v, came, went):
+    parts = [(atm_in.at[r], atm_v.at[r], atm.at[r]) for r in range(ROWS)]
+    parts += [(ocean_in, ocean_v, ocean), (flux_in, flux_v, flux)]
+    ins = [pltpu.make_async_copy(a, v, came.at[i]) for i, (a, v, _) in enumerate(parts)]
+    outs = [pltpu.make_async_copy(v, b, went.at[i]) for i, (_, v, b) in enumerate(parts)]
+    for copy in ins:
+        copy.start()
+    for come, go in zip(ins, outs):
+        come.wait()
+        go.start()
+    for copy in outs:
+        copy.wait()
 
 
 def per_device(
@@ -590,26 +618,23 @@
     surface_heat,
     land_mask,
 ):
-    waves = jnp.pad(wave_of_slot.reshape(NW, 10).T, ((0, 6), (0, 64)))
-    pairs = jnp.stack([pair_dest.reshape(-1), pair_src.reshape(-1), pair_dst.reshape(-1)])
-    pairs = pairs.reshape(3, NW, PAIRS)
     smem = pl.BlockSpec(memory_space=pltpu.SMEM)
     vmem = pl.BlockSpec(memory_space=pltpu.VMEM)
     anys = pl.BlockSpec(memory_space=pl.ANY)
-    return pl.pallas_call(
+    atm, ocean, flux = pl.pallas_call(
         kernel,
         out_shape=(
-            jax.ShapeDtypeStruct((LEV, ROWS, LON), BF16),
+            jax.ShapeDtypeStruct((ROWS, LEV, LON), BF16),
             jax.ShapeDtypeStruct((OLEV, OX, 128), F32),
             jax.ShapeDtypeStruct((OX, 128), F32),
         ),
         in_specs=[smem, smem, vmem, anys, vmem, vmem, vmem, vmem, vmem, anys]
-        + [vmem] * 5,
+        + [vmem] * 7,
         out_specs=(vmem, vmem, vmem),
         scratch_shapes=[
             pltpu.VMEM((LON, LON), BF16),
             pltpu.VMEM((384, LON), BF16),
-            pltpu.VMEM((10, LEV * 16, 128), F32),
+            pltpu.VMEM((10, NW, 128), F32),
             pltpu.VMEM((ND * MSG, 128), F32),
             pltpu.VMEM((ND, MSG, 128), BF16),
             pltpu.VMEM((ND, MSG, 128), BF16),
@@ -628,6 +653,7 @@
             pltpu.VMEM((2, OX, 128), F32),
             pltpu.VMEM((2, EXT, 128), F32),
             pltpu.VMEM((FIELDS, EXT, 256), F32),
+            pltpu.SemaphoreType.REGULAR,
             pltpu.SemaphoreType.DMA((2,)),
             pltpu.SemaphoreType.DMA(()),
             pltpu.SemaphoreType.DMA(()),
@@ -645,20 +671,37 @@
     )(
         wave_of_slot,
         lat_of_row,
-        grid_field,
+        grid_field.transpose(1, 0, 2),
         legendre,
-        waves,
+        wave_of_slot,
         analysis,
         synthesis,
         mode_rates.reshape(1, NLEV),
         flux_weights.reshape(1, NLEV),
         remap_mats,
-        pairs,
+        pair_dest.reshape(NW // 2, 128),
+        pair_src.reshape(NW // 2, 128),
+        pair_dst.reshape(NW // 2, 128),
         ocean_temp,
         diffusivity,
         surface_heat,
         land_mask,
     )
+    atm, ocean, flux = pl.pallas_call(
+        hand_over,
+        out_shape=tuple(jax.ShapeDtypeStruct(v.shape, v.dtype) for v in (atm, ocean, flux)),
+        in_specs=[anys] * 3,
+        out_specs=(anys,) * 3,
+        scratch_shapes=[
+            pltpu.VMEM((ROWS, LEV, LON), BF16),
+            pltpu.VMEM((OLEV, OX, 128), F32),
+            pltpu.VMEM((OX, 128), F32),
+            pltpu.SemaphoreType.DMA((ROWS + 2,)),
+            pltpu.SemaphoreType.DMA((ROWS + 2,)),
+        ],
+        name="hand_over",
+    )(atm, ocean, flux)
+    return atm.transpose(1, 0, 2), ocean, flux
 
 
 def solution(mesh):

time: 102 us -> 91.5 us (0.90)
  local copies, waits for them, and re-layouts: 8.68 us -> 0 us
  other arithmetic: 4.86 us -> 0 us
  Pallas kernels: 86.9 us -> 90.8 us
    unnamed x8 -> x0, local copies, waits for them, and re-layouts: 4.48 us -> none
    unnamed x3 -> x0, other arithmetic: 4.21 us -> none
    pallas_call x1 -> x2, Pallas kernels: 86.9 us -> 90.8 us  [the longest x1 88.6 us: per_device(): pl.pallas_call(kernel, out_shape=(jax.ShapeDtypeStruct((ROWS, LEV, LON),...]
    pallas_call x1 -> x0, local copies, waits for them, and re-layouts: 2.48 us -> none  [per_device(): pl.pallas_call(kernel, out_shape=(jax.ShapeDtypeStruct((LEV, ROWS, LON),...]
where the time goes in v1:
time: 91.5 us; the launch traced here: 91.4 us
  Pallas kernels  90.8 us (99%)
    pallas_call x1, Pallas kernels, per_device(): pl.pallas_call(kernel, out_shape=(jax.ShapeDtypeStruct((ROWS, LEV, LON),...  88.6 us
    pallas_call x1, Pallas kernels, per_device(): pl.pallas_call(hand_over, out_shape=tuple((jax.ShapeDtypeStruct(v.shape,...  2.17 us

profile of v1, /device:TPU:1, one launch (start us, length us, event | category | flops | bytes accessed | tf_op | source)
XLA Modules:
  0.0 91.4 jit_solution(8499300997514874392)
XLA Ops:
  0.6 88.6 %step.1 = (bf16[10,32,1280]{2,1,0:T(8,128)(2,1)}, f32[8,48,128]{2,1,0:T(8,128)}, f32[48,128]{1,0:T(8,128)}) custom-call(s32[640]{0:T(1024)} %wos_v.1, s32[10]{0:T(128)} %lat_s.1, bf16[10,32,1280]{2,1,0:T(8,128)(2,1)} %bitcast.7, bf16[10,640,640]{2,1,0:T(8,128)(2,1)} %legendre.1, s32[640]{0:T(1024)} %wos_v.1, bf16[128,128]{1,0:T(8,128)(2,1)} %analysis.1, ...), custom_call_target="tpu_custom_call" | custom-call | tf_op jit(solution)/shard_map/step/pallas_call | solution.py:624
  89.2 2.2 %hand_over.1 = (bf16[10,32,1280]{2,1,0:T(8,128)(2,1)}, f32[8,48,128]{2,1,0:T(8,128)}, f32[48,128]{1,0:T(8,128)}) custom-call(bf16[10,32,1280]{2,1,0:T(8,128)(2,1)} %get-tuple-element.9.atm_in, f32[8,48,128]{2,1,0:T(8,128)} %get-tuple-element.10.ocean_in, f32[48,128]{1,0:T(8,128)} %get-tuple-element.11.flux_in), custom_call_target="tpu_custom_call" | custom-call | tf_op jit(solution)/shard_map/hand_over/pallas_call | solution.py:690

commit v2 on v1

--- a/solution.py
+++ b/solution.py
@@ -81,7 +81,7 @@
 def kernel(
     wos_s,
     lat_s,
-    field,
+    field_in,
     legendre,
     wos_v,
     analysis,
@@ -99,6 +99,7 @@
     atm,
     ocean,
     flux,
+    field,
     table,
     rows_in,
     waves,
@@ -135,7 +136,11 @@
     w = lax.axis_index("wav")
     me = g * NW + w
     barrier = pltpu.get_barrier_semaphore()
-
+    out3_rows = out3.reshape(NW * 8, 128)
+    in3_rows = in3.reshape(NW * 8, 128)
+
+    field_copy = pltpu.make_async_copy(field_in, field, local_sem.at[2])
+    field_copy.start()
     first_slot = (COLS * g) // 2
     leg_copy = pltpu.make_async_copy(
         legendre.at[pl.ds(first_slot, SLOTS)], leg, local_sem.at[0]
@@ -144,24 +149,17 @@
     mats_copy = pltpu.make_async_copy(mats.at[0], mats_v, local_sem.at[1])
     mats_copy.start()
 
-    low = lax.rem(w, 4)
-    high = w // 4
-    for i in range(NG):
-        for j in range(4):
-            if i or j:
-                pl.semaphore_signal(
-                    barrier,
-                    inc=1,
-                    device_id=(lax.rem(g + i, NG), high * 4 + lax.rem(low + j, 4)),
-                    device_id_type=MESH,
-                )
-    for j in range(1, 16):
-        pl.semaphore_signal(
-            barrier,
-            inc=1,
-            device_id=(g, lax.rem(high + j, 16) * 4 + low),
-            device_id_type=MESH,
-        )
+    outer, inner = w // 8, lax.rem(w, 8)
+    far = [(g, lax.rem(outer + j, 8) * 8 + inner) for j in range(1, 8)]
+    near = [(g, outer * 8 + lax.rem(inner + j, 8)) for j in range(1, 8)]
+    across = [(lax.rem(g + j, NG), w) for j in range(1, NG)]
+
+    def tell(sem, partners):
+        for partner in partners:
+            pl.semaphore_signal(sem, inc=1, device_id=partner, device_id_type=MESH)
+
+    tell(barrier, far + near + across)
+    field_copy.wait()
 
     for r in range(ROWS):
         rows_in[r * LEV : (r + 1) * LEV, :] = field[r]
@@ -218,6 +216,8 @@
         ]
 
     lane64 = lanes((NW, 128))
+    pl.semaphore_wait(barrier, len(far) + len(near) + len(across))
+    tell(ready.at[0], near)
 
     def make_group(i, c):
         gg = lax.rem(g + i, NG)
@@ -236,14 +236,8 @@
                 now, before = twice * now - before, now
         @pl.when(i == 0)
         def _():
-            pl.semaphore_wait(barrier, 30)
-            for j in range(1, 16):
-                pl.semaphore_signal(
-                    ready,
-                    inc=1,
-                    device_id=(g, lax.rem(high + j, 16) * 4 + low),
-                    device_id_type=MESH,
-                )
+            pl.semaphore_wait(ready.at[0], len(near))
+            tell(ready.at[1], across)
 
         out = nt(table[pl.ds(base, COLS * NW), :], rows_in[...])
         start = pl.multiple_of(gg * (NW * MSG), NW * MSG)
@@ -264,7 +258,7 @@
 
         @pl.when(i == 0)
         def _():
-            pl.semaphore_wait(ready, 15)
+            pl.semaphore_wait(ready.at[1], len(across))
             for copy in ocean_copies():
                 copy.start()
             in1[me] = out1[me]
@@ -541,16 +535,16 @@
         parts.append(total)
     products = jnp.concatenate(parts, axis=0)
     for s in range(2):
-        out3[pl.ds(s, NW, stride=8), :] = jnp.dot(
+        out3_rows[pl.ds(s, NW, stride=8), :] = jnp.dot(
             pick_out[s], products, precision=HIGH, preferred_element_type=F32
         )
-    in3[pl.ds(pl.multiple_of(w * 8, 8), 8), :] = out3[pl.ds(pl.multiple_of(w * 8, 8), 8), :]
+    in3[w] = out3[w]
 
     def send_flux(j, c):
         there = lax.rem(w + j, NW)
         pltpu.make_async_remote_copy(
-            src_ref=out3.at[pl.ds(pl.multiple_of(there * 8, 8), 8)],
-            dst_ref=in3.at[pl.ds(pl.multiple_of(w * 8, 8), 8)],
+            src_ref=out3.at[there, pl.ds(0, 2)],
+            dst_ref=in3.at[w, pl.ds(0, 2)],
             send_sem=send3,
             recv_sem=recv3,
             device_id=(g, there),
@@ -568,8 +562,8 @@
             finish(4 * t + q, main[q * LEV : (q + 1) * LEV])
 
     third = pltpu.make_async_remote_copy(
-        src_ref=out3.at[pl.ds(0, (NW - 1) * 8)],
-        dst_ref=in3.at[pl.ds(0, (NW - 1) * 8)],
+        src_ref=out3.at[pl.ds(0, NW - 1), pl.ds(0, 2)],
+        dst_ref=in3.at[pl.ds(0, NW - 1), pl.ds(0, 2)],
         send_sem=send3,
         recv_sem=recv3,
         device_id=(g, w),
@@ -581,7 +575,7 @@
     for half in range(2):
         for s in range(2):
             summed = summed + tn(
-                pick_in[half, s], at(in3, half * 8 + s, NW // 2, 16), HIGH
+                pick_in[half, s], at(in3_rows, half * 8 + s, NW // 2, 16), HIGH
             )
     flux[...] = summed[:OX]
 
@@ -628,10 +622,11 @@
             jax.ShapeDtypeStruct((OLEV, OX, 128), F32),
             jax.ShapeDtypeStruct((OX, 128), F32),
         ),
-        in_specs=[smem, smem, vmem, anys, vmem, vmem, vmem, vmem, vmem, anys]
+        in_specs=[smem, smem, anys, anys, vmem, vmem, vmem, vmem, vmem, anys]
         + [vmem] * 7,
         out_specs=(vmem, vmem, vmem),
         scratch_shapes=[
+            pltpu.VMEM((ROWS, LEV, LON), BF16),
             pltpu.VMEM((LON, LON), BF16),
             pltpu.VMEM((384, LON), BF16),
             pltpu.VMEM((10, NW, 128), F32),
@@ -645,16 +640,16 @@
             pltpu.VMEM((LON, 384), BF16),
             pltpu.VMEM((160, 128), BF16),
             pltpu.VMEM((PAIRS, 128, 128), BF16),
-            pltpu.VMEM((NW * 8, 128), F32),
-            pltpu.VMEM((NW * 8, 128), F32),
+            pltpu.VMEM((NW, 8, 128), F32),
+            pltpu.VMEM((NW, 8, 128), F32),
             pltpu.VMEM((FIELDS, OX, 128), F32),
             pltpu.VMEM((2, FIELDS, HALO, 128), F32),
             pltpu.VMEM((2, FIELDS, HALO, 128), F32),
             pltpu.VMEM((2, OX, 128), F32),
             pltpu.VMEM((2, EXT, 128), F32),
             pltpu.VMEM((FIELDS, EXT, 256), F32),
-            pltpu.SemaphoreType.REGULAR,
-            pltpu.SemaphoreType.DMA((2,)),
+            pltpu.SemaphoreType.REGULAR((2,)),
+            pltpu.SemaphoreType.DMA((3,)),
             pltpu.SemaphoreType.DMA(()),
             pltpu.SemaphoreType.DMA(()),
             pltpu.SemaphoreType.DMA(()),

time: 91.5 us -> 85.9 us (0.939)
  Pallas kernels: 90.8 us -> 85.1 us
    pallas_call x1, Pallas kernels: 88.6 us -> 83 us  [per_device(): pl.pallas_call(kernel, out_shape=(jax.ShapeDtypeStruct((ROWS, LEV, LON),...]
where the time goes in v2:
time: 85.9 us; the launch traced here: 85.8 us
  Pallas kernels  85.1 us (99%)
    pallas_call x1, Pallas kernels, per_device(): pl.pallas_call(kernel, out_shape=(jax.ShapeDtypeStruct((ROWS, LEV, LON),...  83 us
    pallas_call x1, Pallas kernels, per_device(): pl.pallas_call(hand_over, out_shape=tuple((jax.ShapeDtypeStruct(v.shape,...  2.17 us

profile of v2, /device:TPU:1, one launch (start us, length us, event | category | flops | bytes accessed | tf_op | source)
XLA Modules:
  0.0 85.8 jit_solution(2490721565054738913)
XLA Ops:
  0.6 83.0 %step.1 = (bf16[10,32,1280]{2,1,0:T(8,128)(2,1)}, f32[8,48,128]{2,1,0:T(8,128)}, f32[48,128]{1,0:T(8,128)}) custom-call(s32[640]{0:T(1024)} %wos_v.1, s32[10]{0:T(128)} %lat_s.1, bf16[10,32,1280]{2,1,0:T(8,128)(2,1)} %bitcast.7, bf16[10,640,640]{2,1,0:T(8,128)(2,1)} %legendre.1, s32[640]{0:T(1024)} %wos_v.1, bf16[128,128]{1,0:T(8,128)(2,1)} %analysis.1, ...), custom_call_target="tpu_custom_call" | custom-call | tf_op jit(solution)/shard_map/step/pallas_call | solution.py:618
  83.6 2.2 %hand_over.1 = (bf16[10,32,1280]{2,1,0:T(8,128)(2,1)}, f32[8,48,128]{2,1,0:T(8,128)}, f32[48,128]{1,0:T(8,128)}) custom-call(bf16[10,32,1280]{2,1,0:T(8,128)(2,1)} %get-tuple-element.9.atm_in, f32[8,48,128]{2,1,0:T(8,128)} %get-tuple-element.10.ocean_in, f32[48,128]{1,0:T(8,128)} %get-tuple-element.11.flux_in), custom_call_target="tpu_custom_call" | custom-call | tf_op jit(solution)/shard_map/hand_over/pallas_call | solution.py:685

commit v3 on v2

--- a/solution.py
+++ b/solution.py
@@ -408,8 +408,8 @@
 
     odd = lax.rem(g, 2)
 
-    def column(cl, c):
-        here = pl.ds(pl.multiple_of(cl * WAVES, WAVES), WAVES)
+    for cl in range(COLS):
+        here = pl.ds(cl * WAVES, WAVES)
         table_of = leg[(odd + cl) // 2]
         m = wos_s[w * 10 + (COLS * g + cl) // 2]
         spectra = jnp.dot(
@@ -436,9 +436,6 @@
         back = nt(table_of, right)
         cols_f[here, :] = back[:, :128]
         flux_f[here, :] = back[:, 128:]
-        return c
-
-    lax.fori_loop(0, COLS, column, 0)
 
     for cl in range(COLS):
         for t in range(2):
@@ -498,10 +495,6 @@
         f12 = at(acc, k * NW * MSG + 12, NW, MSG)
         for cl in range(COLS):
             rows = pl.ds((k * COLS + cl) * NW, NW)
-            for t in range(2):
-                lhs[rows, t * 128 : (t + 1) * 128] = at(
-                    acc, k * NW * MSG + 2 * cl + t, NW, MSG
-                ).astype(BF16)
             v = at(acc, k * NW * MSG + 10 + cl // 2, NW, MSG) if cl < 4 else f12
             if cl % 2 == 1:
                 v = pltpu.roll(v, 64, 1)
@@ -556,6 +549,12 @@
 
     for r in range(2):
         finish(8 + r, last[r * LEV : (r + 1) * LEV])
+    for k in range(NG):
+        for cl in range(COLS):
+            for t in range(2):
+                lhs[pl.ds((k * COLS + cl) * NW, NW), t * 128 : (t + 1) * 128] = at(
+                    acc, k * NW * MSG + 2 * cl + t, NW, MSG
+                ).astype(BF16)
     for t in range(2):
         main = tn(lhs[:, t * 128 : (t + 1) * 128], table[...])
         for q in range(4):

time: 85.9 us -> 81.1 us (0.944)
  Pallas kernels: 85.1 us -> 80.4 us
    pallas_call x1, Pallas kernels: 83 us -> 78.2 us  [per_device(): pl.pallas_call(kernel, out_shape=(jax.ShapeDtypeStruct((ROWS, LEV, LON),...]
where the time goes in v3:
time: 81.1 us; the launch traced here: 81 us
  Pallas kernels  80.4 us (99%)
    pallas_call x1, Pallas kernels, per_device(): pl.pallas_call(kernel, out_shape=(jax.ShapeDtypeStruct((ROWS, LEV, LON),...  78.2 us
    pallas_call x1, Pallas kernels, per_device(): pl.pallas_call(hand_over, out_shape=tuple((jax.ShapeDtypeStruct(v.shape,...  2.17 us

profile of v3, /device:TPU:1, one launch (start us, length us, event | category | flops | bytes accessed | tf_op | source)
XLA Modules:
  0.0 81.0 jit_solution(3827005006762484782)
XLA Ops:
  0.6 78.2 %step.1 = (bf16[10,32,1280]{2,1,0:T(8,128)(2,1)}, f32[8,48,128]{2,1,0:T(8,128)}, f32[48,128]{1,0:T(8,128)}) custom-call(s32[640]{0:T(1024)} %wos_v.1, s32[10]{0:T(128)} %lat_s.1, bf16[10,32,1280]{2,1,0:T(8,128)(2,1)} %bitcast.7, bf16[10,640,640]{2,1,0:T(8,128)(2,1)} %legendre.1, s32[640]{0:T(1024)} %wos_v.1, bf16[128,128]{1,0:T(8,128)(2,1)} %analysis.1, ...), custom_call_target="tpu_custom_call" | custom-call | tf_op jit(solution)/shard_map/step/pallas_call | solution.py:617
  78.8 2.2 %hand_over.1 = (bf16[10,32,1280]{2,1,0:T(8,128)(2,1)}, f32[8,48,128]{2,1,0:T(8,128)}, f32[48,128]{1,0:T(8,128)}) custom-call(bf16[10,32,1280]{2,1,0:T(8,128)(2,1)} %get-tuple-element.9.atm_in, f32[8,48,128]{2,1,0:T(8,128)} %get-tuple-element.10.ocean_in, f32[48,128]{1,0:T(8,128)} %get-tuple-element.11.flux_in), custom_call_target="tpu_custom_call" | custom-call | tf_op jit(solution)/shard_map/hand_over/pallas_call | solution.py:684
